TPU v7x, 32 devices: a whole 2x2x4 slice. The times are simulated.
32 devices in a mesh: region: 4 (over y, core), shard: 8 (over z, x).
Axes of the slice: x: 2, y: 2, z: 4, core: 2. Of those that a mesh axis runs over, the one named last changes fastest.
Arguments:
- fields: bfloat16 [32, 16384], P('shard', 'region'), may hold values from -6 to 6
- near_coef: bfloat16 [128, 3, 128, 128], P(('region', 'shard')), may hold values from -0.25 to 0.25
- far_coef: bfloat16 [128, 2, 128, 128], P(('region', 'shard')), may hold values from -0.25 to 0.25
- inv_factor: bfloat16 [128, 128, 128], P(('region', 'shard')), as said below
- near_block: int32 [128, 3], P(('region', 'shard')), may hold values from 0 to 3, as said below
- far_region: int32 [128, 2], P(('region', 'shard')), may hold values from 0 to 3, all different within a row; in each aligned block of 4 rows (0 to 3, 4 to 7, ...) at most 2 rows name the same one
- far_block: int32 [128, 2], P(('region', 'shard')), may hold values from 0 to 3
Outputs:
- whitened: bfloat16 [32, 16384], P('shard', 'region')
Inputs may be any that keep to these rules, and one draw needn't show every extreme that they name: inv_factor[g] is upper triangular with a positive diagonal. `near_block`: row g lists 3 different indices of its own group of 4 blocks, never g % 4 itself. `far_region`: each row names 2 different regions; within the rows of one group of 4 blocks no region is named more than 2 times.
All inputs are finite; a program needn't handle non-finite values.
Results may differ from a plain program's by a relative error of at most 0.0049.
Values may be sent and summed in bfloat16 or wider, within the bound.
A program may use at most 64 MiB of HBM per device.

v0:
```python
import jax
import jax.numpy as jnp
from jax import lax
from jax.sharding import PartitionSpec as P


def rank_within(regions):
    entries = regions.shape[-1]
    identical = regions[..., :, None] == regions[..., None, :]
    earlier = jnp.arange(entries)[None, :] < jnp.arange(entries)[:, None]
    return jnp.sum(jnp.logical_and(identical, earlier), axis=-1)


def slot_sources(regions, blocks, target, capacity):
    rank_list = rank_within(regions)
    wanted = jnp.logical_and(
        (regions == target)[..., :, None], rank_list[..., :, None] == jnp.arange(capacity)
    )
    return jnp.sum(jnp.where(wanted, blocks[..., :, None], 0), axis=-2)


def selector(indices, count):
    return (indices[..., None] == jnp.arange(count, dtype=jnp.int32)).astype(jnp.bfloat16)


def body(fields, near_coef, far_coef, inv_factor, near_block, far_region, far_block):
    samp_rows = fields.shape[0]
    shard_count = lax.axis_size("shard")
    region_count = lax.axis_size("region")
    blocks_here, far_count = far_region.shape
    block_width = near_coef.shape[-1]
    entries = blocks_here * far_count
    capacity = max(2, -(-entries // region_count))
    slot_count = region_count * capacity
    own_region = lax.axis_index("region")
    flat_regions = far_region.reshape(entries)
    own_slots = flat_regions * capacity + rank_within(flat_regions)
    wanted_regions, wanted_blocks = (
        lax.all_gather(far_region, ("region", "shard"), axis=0, tiled=True),
        lax.all_gather(far_block, ("region", "shard"), axis=0, tiled=True),
    )
    sources = slot_sources(
        wanted_regions.reshape(region_count, shard_count, entries),
        wanted_blocks.reshape(region_count, shard_count, entries),
        own_region,
        capacity,
    )
    sources = jnp.transpose(sources, (1, 0, 2)).reshape(shard_count, slot_count)
    pick_send = selector(sources, blocks_here)
    sample_view = fields.reshape(samp_rows, shard_count, blocks_here, block_width)
    outgoing = jnp.einsum(
        "sgbd,gcb->sgcd", sample_view, pick_send, preferred_element_type=jnp.float32
    ).astype(jnp.bfloat16)
    outgoing = outgoing.reshape(samp_rows, shard_count, slot_count * block_width)
    arrived = lax.all_to_all(outgoing, "region", split_axis=2, concat_axis=2, tiled=True)
    combined = jnp.concatenate(
        [fields.reshape(samp_rows, shard_count, blocks_here * block_width), arrived], axis=2
    )
    transposed = lax.all_to_all(combined, "shard", split_axis=1, concat_axis=0, tiled=True)
    total_rows = transposed.shape[0]
    block_data = transposed[:, 0, : blocks_here * block_width].reshape(
        total_rows, blocks_here, block_width
    )
    incoming = transposed[:, 0, blocks_here * block_width :].reshape(
        total_rows, slot_count, block_width
    )
    pick_far = selector(own_slots, slot_count)
    far_data = jnp.einsum(
        "scd,ec->sed", incoming, pick_far, preferred_element_type=jnp.float32
    ).astype(jnp.bfloat16)
    far_data = far_data.reshape(total_rows, blocks_here, far_count, block_width)
    pick_near = selector(near_block, blocks_here)
    near_data = jnp.einsum(
        "skd,bjk->sbjd", block_data, pick_near, preferred_element_type=jnp.float32
    ).astype(jnp.bfloat16)
    cond_mean = jnp.einsum(
        "sbjd,bjde->sbe", near_data, near_coef, preferred_element_type=jnp.float32
    )
    cond_mean = cond_mean + jnp.einsum(
        "sbjd,bjde->sbe", far_data, far_coef, preferred_element_type=jnp.float32
    )
    residual = (block_data.astype(jnp.float32) - cond_mean).astype(jnp.bfloat16)
    whitened = jnp.einsum(
        "sbd,bde->sbe", residual, inv_factor, preferred_element_type=jnp.float32
    ).astype(jnp.bfloat16)
    whitened = whitened.reshape(total_rows, blocks_here * block_width)
    return lax.all_to_all(whitened, "shard", split_axis=0, concat_axis=1, tiled=True)


def solution(mesh):
    return jax.shard_map(
        body,
        mesh=mesh,
        in_specs=(
            P("shard", "region"),
            P(("region", "shard"), None, None, None),
            P(("region", "shard"), None, None, None),
            P(("region", "shard"), None, None),
            P(("region", "shard"), None),
            P(("region", "shard"), None),
            P(("region", "shard"), None),
        ),
        out_specs=P("shard", "region"),
        check_vma=False,
    )
```

profile of v0, /device:TPU:0, one launch (start us, length us, event | category | flops | bytes accessed | tf_op | source)
XLA Modules:
  0.0 177.2 jit_solution(17149873583715637292)
XLA Ops:
  0.0 0.0 copy-start
  0.0 0.0 copy-start.4
  0.0 0.0 copy-start.2
  0.0 70.1 %all-gather = s32[32,4,2]{1,2,0:T(2,128)S(1)} all-gather(s32[1,4,2]{1,2,0:T(2,128)} %bitcast.97), channel_id=1, replica_groups=mesh['region'=4,'shard'=8] {'region','shard'}, dimensions={0}, use_global_device_ids=true | all-gather | bytes 1056 | tf_op jit(solution)/shard_map/all_gather | solution.py:39
  70.1 0.1 copy.72
  70.2 0.1 reshape.57
  70.3 0.1 copy.74
  70.4 0.1 copy.73
  70.5 63.7 %all-gather.1 = s32[32,4,2]{1,2,0:T(2,128)S(1)} all-gather(s32[1,4,2]{1,2,0:T(2,128)} %bitcast.98), channel_id=1, replica_groups=mesh['region'=4,'shard'=8] {'region','shard'}, dimensions={0}, use_global_device_ids=true | all-gather | bytes 1056 | tf_op jit(solution)/shard_map/all_gather | solution.py:40
  134.2 0.1 copy.76
  134.3 0.1 broadcast_in_dim.10
  134.4 0.1 copy.77
  134.4 0.7 convert_reduce_fusion
  135.1 0.2 select_reduce_fusion
  135.4 0.1 copy.78
  135.4 0.8 reshape.58
  136.2 0.2 fusion.1
  136.4 0.5 copy.92
  137.0 1.7 reshape.75
  138.7 3.3 %all-to-all-start = ((bf16[4,2,4096]{2,1,0:T(2,128)(2,1)}), bf16[4,2,4096]{2,1,0:T(2,128)(2,1)S(1)}, u32[]{:S(2)}, u32[]{:S(2)}) async-start(bf16[4,2,4096]{2,1,0:T(2,128)(2,1)} %reshape.75), calls=%async_computation | async-start | bytes 131072 | tf_op jit(solution)/shard_map/all_to_all | solution.py:55
  142.0 0.0 copy-done.4
  142.0 0.1 copy.85
  142.1 0.1 reshape.60
  142.2 0.2 convert_reduce_fusion.1
  142.4 0.0 copy-done.2
  142.4 0.3 copy.81
  142.7 3.4 %all-to-all-done = bf16[4,2,4096]{2,1,0:T(2,128)(2,1)S(1)} async-done(((bf16[4,2,4096]{2,1,0:T(2,128)(2,1)}), bf16[4,2,4096]{2,1,0:T(2,128)(2,1)S(1)}, u32[]{:S(2)}, u32[]{:S(2)}) %all-to-all-start) | async-done | bytes 65568 | tf_op jit(solution)/shard_map/all_to_all | solution.py:55
  146.1 1.2 reshape.76
  147.3 6.6 %pad_maximum_fusion = bf16[4,8,1536]{1,0,2:T(4,128)(2,1)S(1)} fusion(bf16[4,8,1024]{1,0,2:T(4,128)(2,1)S(1)} %bitcast.86, bf16[4,8,512]{1,0,2:T(4,128)(2,1)S(1)} %copy.81), kind=kLoop, calls=%fused_computation | loop fusion | flops 49152 | bytes 196608 | tf_op jit(solution)/shard_map/concatenate | solution.py:56
  153.9 0.0 copy-start.5
  153.9 0.0 copy-start.1
  153.9 0.0 copy-start.3
  153.9 1.8 %copy.82 = bf16[4,8,1536]{2,0,1:T(4,128)(2,1)} copy(bf16[4,8,1536]{1,0,2:T(4,128)(2,1)S(1)} %pad_maximum_fusion) | data formatting | bytes 196608 | tf_op jit(solution)/shard_map/concatenate | solution.py:56
  155.7 3.5 %all-to-all-start.1 = ((bf16[4,8,1536]{2,0,1:T(4,128)(2,1)}), bf16[4,8,1536]{2,0,1:T(4,128)(2,1)S(1)}, u32[]{:S(2)}, u32[]{:S(2)}) async-start(bf16[4,8,1536]{2,0,1:T(4,128)(2,1)} %copy.82), calls=%async_computation.1 | async-start | bytes 196608 | tf_op jit(solution)/shard_map/all_to_all | solution.py:59
  159.2 7.1 %all-to-all-done.1 = bf16[4,8,1536]{2,0,1:T(4,128)(2,1)S(1)} async-done(((bf16[4,8,1536]{2,0,1:T(4,128)(2,1)}), bf16[4,8,1536]{2,0,1:T(4,128)(2,1)S(1)}, u32[]{:S(2)}, u32[]{:S(2)}) %all-to-all-start.1) | async-done | bytes 98336 | tf_op jit(solution)/shard_map/all_to_all | solution.py:59
  166.5 0.2 convolution_convert_fusion.1
  166.7 0.0 copy-done.5
  166.7 0.2 fusion
  166.9 0.0 copy-done
  166.9 0.2 convolution_bitcast_fusion.1
  167.1 0.0 copy-done.1
  167.1 0.0 copy-done.3
  167.1 0.3 fusion.6
  167.5 9.1 %all_to_all.42 = bf16[8,4,512]{2,1,0:T(4,128)(2,1)S(1)} all-to-all(bf16[8,4,512]{2,1,0:T(4,128)(2,1)S(1)} %all_to_all.35), channel_id=1, replica_groups=mesh['region'=4,'shard'=8] {'shard'}, dimensions={0} | all-to-all | bytes 65536 | tf_op jit(solution)/shard_map/all_to_all | solution.py:87
  176.5 0.6 copy.109
  (12 shorter events, 0.2 us)
Async XLA Ops:
  0.0 166.9 %copy-start = (bf16[4,3,128,128]{3,2,1,0:T(8,128)(2,1)S(1)}, bf16[4,3,128,128]{3,2,1,0:T(8,128)(2,1)}, u32[]{:S(2)}) copy-start(bf16[4,3,128,128]{3,2,1,0:T(8,128)(2,1)} %param.8) | copy-start | bytes 1179652
  0.0 142.0 %copy-start.4 = (s32[4,2]{0,1:T(2,128)S(1)}, s32[4,2]{0,1:T(2,128)}, u32[]{:S(2)}) copy-start(s32[4,2]{0,1:T(2,128)} %param.12) | copy-start | bytes 100
  0.0 142.4 %copy-start.2 = (bf16[4,4096]{1,0:T(4,128)(2,1)S(1)}, bf16[4,4096]{1,0:T(4,128)(2,1)}, u32[]{:S(2)}) copy-start(bf16[4,4096]{1,0:T(4,128)(2,1)} %param.7) | copy-start | bytes 98308
  138.7 7.4 %all-to-all-start = ((bf16[4,2,4096]{2,1,0:T(2,128)(2,1)}), bf16[4,2,4096]{2,1,0:T(2,128)(2,1)S(1)}, u32[]{:S(2)}, u32[]{:S(2)}) async-start(bf16[4,2,4096]{2,1,0:T(2,128)(2,1)} %reshape.75), calls=%async_computation | async-start | bytes 131072 | tf_op jit(solution)/shard_map/all_to_all | solution.py:55
  153.9 12.8 %copy-start.5 = (s32[4,3]{1,0:T(4,128)S(1)}, s32[4,3]{1,0:T(4,128)}, u32[]{:S(2)}) copy-start(s32[4,3]{1,0:T(4,128)} %param.11) | copy-start | bytes 148
  153.9 13.2 %copy-start.1 = (bf16[4,2,128,128]{3,2,1,0:T(8,128)(2,1)S(1)}, bf16[4,2,128,128]{3,2,1,0:T(8,128)(2,1)}, u32[]{:S(2)}) copy-start(bf16[4,2,128,128]{3,2,1,0:T(8,128)(2,1)} %param.9) | copy-start | bytes 786436
  153.9 13.2 %copy-start.3 = (bf16[4,128,128]{2,1,0:T(8,128)(2,1)S(1)}, bf16[4,128,128]{2,1,0:T(8,128)(2,1)}, u32[]{:S(2)}) copy-start(bf16[4,128,128]{2,1,0:T(8,128)(2,1)} %param.10) | copy-start | bytes 393220
  155.7 10.6 %all-to-all-start.1 = ((bf16[4,8,1536]{2,0,1:T(4,128)(2,1)}), bf16[4,8,1536]{2,0,1:T(4,128)(2,1)S(1)}, u32[]{:S(2)}, u32[]{:S(2)}) async-start(bf16[4,8,1536]{2,0,1:T(4,128)(2,1)} %copy.82), calls=%async_computation.1 | async-start | bytes 196608 | tf_op jit(solution)/shard_map/all_to_all | solution.py:59
where the time goes:
time: 178 us; the launch traced here: 177 us
  blocking collectives  143 us (80%)
  waiting for transfers between devices  10.5 us (6%)
  local copies, waits for them, and re-layouts  8.01 us (4%)
  other arithmetic  7.7 us (4%)
  starting transfers between devices  6.77 us (4%)
    all_gather x1, blocking collectives, body(): lax.all_gather(far_region, ('region', 'shard'), axis=0, tiled=True)  70.1 us
    all_gather x1, blocking collectives, body(): lax.all_gather(far_block, ('region', 'shard'), axis=0, tiled=True)  63.7 us
    all_to_all x1, blocking collectives, body(): lax.all_to_all(whitened, 'shard', split_axis=0, concat_axis=1, tiled=True)  9.06 us
    all_to_all x1, waiting for transfers between devices, body(): lax.all_to_all(combined, 'shard', split_axis=1, concat_axis=0, tiled=True)  7.12 us
    concatenate x1, other arithmetic, body(): jnp.concatenate([fields.reshape(samp_rows, shard_count, blocks_here * blo...  6.58 us
    unnamed x19, local copies, waits for them, and re-layouts  3.67 us
  transfers between devices with their start and end apart: 2, of which 2 were waited for; matrix products, arithmetic and copies ran while one was open for 0% of the time, Pallas kernels for 0%

commit v1 on v0

--- a/solution.py
+++ b/solution.py
@@ -2,6 +2,18 @@
 import jax.numpy as jnp
 from jax import lax
 from jax.sharding import PartitionSpec as P
+
+
+def collect(x, axis, dim):
+    ways, here = (lax.axis_size(axis), lax.axis_index(axis))
+    grown, reach = (x, 1)
+    while reach < ways:
+        theirs = lax.ppermute(grown, axis, [(d, d ^ reach) for d in range(ways)])
+        mine_first = jnp.concatenate([grown, theirs], axis=dim)
+        theirs_first = jnp.concatenate([theirs, grown], axis=dim)
+        grown = jnp.where(here & reach == 0, mine_first, theirs_first)
+        reach = 2 * reach
+    return grown
 
 
 def rank_within(regions):
@@ -37,7 +49,7 @@
     own_slots = flat_regions * capacity + rank_within(flat_regions)
     wanted_regions, wanted_blocks = (
         lax.all_gather(far_region, ("region", "shard"), axis=0, tiled=True),
-        lax.all_gather(far_block, ("region", "shard"), axis=0, tiled=True),
+        collect(far_block, ("region", "shard"), 0),
     )
     sources = slot_sources(
         wanted_regions.reshape(region_count, shard_count, entries),

time: 178 us -> 126 us (0.71)
  blocking collectives: 143 us -> 76.3 us
  waiting for transfers between devices: 10.5 us -> 20.3 us
  starting transfers between devices: 6.77 us -> 10.1 us
    all_gather x1 -> x0, blocking collectives: 63.7 us -> none  [body(): lax.all_gather(far_block, ('region', 'shard'), axis=0, tiled=True)]
    ppermute x0 -> x5, waiting for transfers between devices: none -> 9.66 us  [collect(): theirs = lax.ppermute(grown, axis, [(d, d ^ reach) for d in range(ways)])]
    ppermute x0 -> x5, starting transfers between devices: none -> 3.47 us  [collect(): theirs = lax.ppermute(grown, axis, [(d, d ^ reach) for d in range(ways)])]
    all_gather x1, blocking collectives: 70.1 us -> 67.3 us  [body(): lax.all_gather(far_region, ('region', 'shard'), axis=0, tiled=True)]
    unnamed x19 -> x17, local copies, waits for them, and re-layouts: 3.67 us -> 4.34 us
  transfers between devices with their start and end apart: 2 -> 7, of which waited for: 2 -> 6; matrix products, arithmetic and copies ran while one was open for 0% -> 3% of each run, Pallas kernels for 0% -> 0%
where the time goes in v1:
time: 126 us
  blocking collectives  76.3 us (61%)
  waiting for transfers between devices  20.3 us (16%)
  starting transfers between devices  10.1 us (8%)
  other arithmetic  8.83 us (7%)
  local copies, waits for them, and re-layouts  8.63 us (7%)
    all_gather x1, blocking collectives, body(): lax.all_gather(far_region, ('region', 'shard'), axis=0, tiled=True)  67.3 us
    ppermute x5, waiting for transfers between devices, collect(): theirs = lax.ppermute(grown, axis, [(d, d ^ reach) for d in range(ways)])  9.66 us
    all_to_all x1, blocking collectives, body(): lax.all_to_all(whitened, 'shard', split_axis=0, concat_axis=1, tiled=True)  9.06 us
    all_to_all x1, waiting for transfers between devices, body(): lax.all_to_all(combined, 'shard', split_axis=1, concat_axis=0, tiled=True)  7.05 us
    concatenate x1, other arithmetic, body(): jnp.concatenate([fields.reshape(samp_rows, shard_count, blocks_here * blo...  6.58 us
    unnamed x17, local copies, waits for them, and re-layouts  4.34 us
    all_to_all x1, waiting for transfers between devices, body(): lax.all_to_all(outgoing, 'region', split_axis=2, concat_axis=2, tiled=True)  3.57 us
    ppermute x5, starting transfers between devices, collect(): theirs = lax.ppermute(grown, axis, [(d, d ^ reach) for d in range(ways)])  3.47 us
  transfers between devices with their start and end apart: 7, of which 6 were waited for; matrix products, arithmetic and copies ran while one was open for 3% of the time, Pallas kernels for 0%

profile of v1, /device:TPU:0, one launch (start us, length us, event | category | flops | bytes accessed | tf_op | source)
XLA Modules:
  0.0 125.6 jit_solution(7724691764582182588)
XLA Ops:
  0.0 0.0 copy-start
  0.0 0.0 copy-start.2
  0.0 2.9 %collective-permute-start = (s32[4,2]{0,1:T(2,128)}, s32[4,2]{0,1:T(2,128)S(1)}, u32[]{:S(2)}, u32[]{:S(2)}) collective-permute-start(s32[4,2]{0,1:T(2,128)} %param.13), channel_id=1, source_target_pairs={{0,1},{1,0},{2,3},{3,2},{4,5},{5,4},{6,7},{7,6},{8,9},{9,8},{10,11... | collective-permute-start | bytes 104 | tf_op jit(solution)/shard_map/ppermute | solution.py:11
  2.9 67.3 %all-gather = s32[32,4,2]{1,2,0:T(2,128)S(1)} all-gather(s32[1,4,2]{1,2,0:T(2,128)} %bitcast.94), channel_id=1, replica_groups=mesh['region'=4,'shard'=8] {'region','shard'}, dimensions={0}, use_global_device_ids=true | all-gather | bytes 1056 | tf_op jit(solution)/shard_map/all_gather | solution.py:51
  70.2 0.1 copy.68
  70.3 0.1 reshape.67
  70.4 0.0 collective-permute-done
  70.4 0.8 add_select_fusion
  71.3 0.0 collective-permute-start.1
  71.3 3.5 %collective-permute-done.1 = s32[8,2]{0,1:T(2,128)S(1)} collective-permute-done((s32[8,2]{0,1:T(2,128)S(1)}, s32[8,2]{0,1:T(2,128)S(1)}, u32[]{:S(2)}, u32[]{:S(2)}) %collective-permute-start.1) | collective-permute-done | bytes 96 | tf_op jit(solution)/shard_map/ppermute | solution.py:11
  74.8 0.1 add_select_fusion.1
  74.9 0.0 collective-permute-start.2
  74.9 4.4 %collective-permute-done.2 = s32[16,2]{0,1:T(2,128)S(1)} collective-permute-done((s32[16,2]{0,1:T(2,128)S(1)}, s32[16,2]{0,1:T(2,128)S(1)}, u32[]{:S(2)}, u32[]{:S(2)}) %collective-permute-start.2) | collective-permute-done | bytes 160 | tf_op jit(solution)/shard_map/ppermute | solution.py:11
  79.4 0.1 add_select_fusion.2
  79.5 0.0 collective-permute-start.3
  79.5 0.1 copy.70
  79.6 1.0 collective-permute-done.3
  80.6 0.1 add_select_fusion.3
  80.7 0.5 collective-permute-start.4
  81.2 0.7 convert_reduce_fusion
  81.9 0.8 copy.80
  82.6 0.1 copy.69
  82.7 0.8 reshape.68
  83.5 0.1 reshape.70
  83.6 0.6 collective-permute-done.4
  84.2 0.1 add_select_fusion.4
  84.3 0.1 copy.72
  84.4 0.1 select_n.61
  84.5 0.2 select_reduce_fusion
  84.7 0.1 copy.73
  84.8 0.2 fusion.1
  85.0 0.5 copy.87
  85.6 1.7 %reshape.82 = bf16[4,2,4096]{2,1,0:T(2,128)(2,1)} reshape(bf16[1024,4,8]{2,1,0:T(4,128)(2,1)S(1)} %bitcast.84) | data formatting | bytes 131072
  87.3 3.3 %all-to-all-start = ((bf16[4,2,4096]{2,1,0:T(2,128)(2,1)}), bf16[4,2,4096]{2,1,0:T(2,128)(2,1)S(1)}, u32[]{:S(2)}, u32[]{:S(2)}) async-start(bf16[4,2,4096]{2,1,0:T(2,128)(2,1)} %reshape.82), calls=%async_computation | async-start | bytes 131072 | tf_op jit(solution)/shard_map/all_to_all | solution.py:67
  90.6 0.2 convert_reduce_fusion.1
  90.8 0.0 copy-done.2
  90.8 0.3 copy.76
  91.1 3.6 %all-to-all-done = bf16[4,2,4096]{2,1,0:T(2,128)(2,1)S(1)} async-done(((bf16[4,2,4096]{2,1,0:T(2,128)(2,1)}), bf16[4,2,4096]{2,1,0:T(2,128)(2,1)S(1)}, u32[]{:S(2)}, u32[]{:S(2)}) %all-to-all-start) | async-done | bytes 65568 | tf_op jit(solution)/shard_map/all_to_all | solution.py:67
  94.7 1.2 reshape.83
  95.9 6.6 %pad_maximum_fusion = bf16[4,8,1536]{1,0,2:T(4,128)(2,1)S(1)} fusion(bf16[4,8,1024]{1,0,2:T(4,128)(2,1)S(1)} %bitcast.83, bf16[4,8,512]{1,0,2:T(4,128)(2,1)S(1)} %copy.76), kind=kLoop, calls=%fused_computation | loop fusion | flops 49152 | bytes 196608 | tf_op jit(solution)/shard_map/concatenate | solution.py:68
  102.5 0.0 copy-start.4
  102.5 0.0 copy-start.1
  102.5 0.0 copy-start.3
  102.5 1.8 %copy.77 = bf16[4,8,1536]{2,0,1:T(4,128)(2,1)} copy(bf16[4,8,1536]{1,0,2:T(4,128)(2,1)S(1)} %pad_maximum_fusion) | data formatting | bytes 196608 | tf_op jit(solution)/shard_map/concatenate | solution.py:68
  104.3 3.4 %all-to-all-start.1 = ((bf16[4,8,1536]{2,0,1:T(4,128)(2,1)}), bf16[4,8,1536]{2,0,1:T(4,128)(2,1)S(1)}, u32[]{:S(2)}, u32[]{:S(2)}) async-start(bf16[4,8,1536]{2,0,1:T(4,128)(2,1)} %copy.77), calls=%async_computation.1 | async-start | bytes 196608 | tf_op jit(solution)/shard_map/all_to_all | solution.py:71
  107.7 7.0 %all-to-all-done.1 = bf16[4,8,1536]{2,0,1:T(4,128)(2,1)S(1)} async-done(((bf16[4,8,1536]{2,0,1:T(4,128)(2,1)}), bf16[4,8,1536]{2,0,1:T(4,128)(2,1)S(1)}, u32[]{:S(2)}, u32[]{:S(2)}) %all-to-all-start.1) | async-done | bytes 98336 | tf_op jit(solution)/shard_map/all_to_all | solution.py:71
  114.9 0.0 copy-done.4
  114.9 0.2 fusion
  115.1 0.0 copy-done
  115.1 0.2 convolution_bitcast_fusion.1
  115.3 0.2 convolution_convert_fusion.1
  115.5 0.0 copy-done.1
  115.6 0.0 copy-done.3
  115.6 0.3 fusion.6
  115.9 9.1 %all_to_all.42 = bf16[8,4,512]{2,1,0:T(4,128)(2,1)S(1)} all-to-all(bf16[8,4,512]{2,1,0:T(4,128)(2,1)S(1)} %all_to_all.35), channel_id=1, replica_groups=mesh['region'=4,'shard'=8] {'shard'}, dimensions={0} | all-to-all | bytes 65536 | tf_op jit(solution)/shard_map/all_to_all | solution.py:99
  125.0 0.6 copy.104
  (12 shorter events, 0.2 us)
Async XLA Ops:
  0.0 115.1 %copy-start = (bf16[4,3,128,128]{3,2,1,0:T(8,128)(2,1)S(1)}, bf16[4,3,128,128]{3,2,1,0:T(8,128)(2,1)}, u32[]{:S(2)}) copy-start(bf16[4,3,128,128]{3,2,1,0:T(8,128)(2,1)} %param.8) | copy-start | bytes 1179652
  0.0 90.8 %copy-start.2 = (bf16[4,4096]{1,0:T(4,128)(2,1)S(1)}, bf16[4,4096]{1,0:T(4,128)(2,1)}, u32[]{:S(2)}) copy-start(bf16[4,4096]{1,0:T(4,128)(2,1)} %param.7) | copy-start | bytes 98308
  0.0 70.4 %collective-permute-start = (s32[4,2]{0,1:T(2,128)}, s32[4,2]{0,1:T(2,128)S(1)}, u32[]{:S(2)}, u32[]{:S(2)}) collective-permute-start(s32[4,2]{0,1:T(2,128)} %param.13), channel_id=1, source_target_pairs={{0,1},{1,0},{2,3},{3,2},{4,5},{5,4},{6,7},{7,6},{8,9},{9,8},{10,11... | collective-permute-start | bytes 104 | tf_op jit(solution)/shard_map/ppermute | solution.py:11
  71.3 3.6 %collective-permute-start.1 = (s32[8,2]{0,1:T(2,128)S(1)}, s32[8,2]{0,1:T(2,128)S(1)}, u32[]{:S(2)}, u32[]{:S(2)}) collective-permute-start(s32[8,2]{0,1:T(2,128)S(1)} %add_select_fusion), channel_id=1, source_target_pairs={{0,2},{1,3},{2,0},{3,1},{4,6},{5,7},{6,4},{7,5},{8,10},{9,11},{10,... | collective-permute-start | bytes 200 | tf_op jit(solution)/shard_map/ppermute | solution.py:11
  74.9 4.5 %collective-permute-start.2 = (s32[16,2]{0,1:T(2,128)S(1)}, s32[16,2]{0,1:T(2,128)S(1)}, u32[]{:S(2)}, u32[]{:S(2)}) collective-permute-start(s32[16,2]{0,1:T(2,128)S(1)} %add_select_fusion.1), channel_id=1, source_target_pairs={{0,4},{1,5},{2,6},{3,7},{4,0},{5,1},{6,2},{7,3},{8,12},{9,13},{10,... | collective-permute-start | bytes 392 | tf_op jit(solution)/shard_map/ppermute | solution.py:11
  79.5 1.1 collective-permute-start.3
  80.7 3.6 %collective-permute-start.4 = (s32[64,2]{0,1:T(2,128)S(1)}, s32[64,2]{0,1:T(2,128)S(1)}, u32[]{:S(2)}, u32[]{:S(2)}) collective-permute-start(s32[64,2]{0,1:T(2,128)S(1)} %add_select_fusion.3), channel_id=1, source_target_pairs={{0,16},{1,17},{2,18},{3,19},{4,20},{5,21},{6,22},{7,23},{8,24},{9,... | collective-permute-start | bytes 1544 | tf_op jit(solution)/shard_map/ppermute | solution.py:11
  87.3 7.4 %all-to-all-start = ((bf16[4,2,4096]{2,1,0:T(2,128)(2,1)}), bf16[4,2,4096]{2,1,0:T(2,128)(2,1)S(1)}, u32[]{:S(2)}, u32[]{:S(2)}) async-start(bf16[4,2,4096]{2,1,0:T(2,128)(2,1)} %reshape.82), calls=%async_computation | async-start | bytes 131072 | tf_op jit(solution)/shard_map/all_to_all | solution.py:67
  102.5 12.4 %copy-start.4 = (s32[4,3]{1,0:T(4,128)S(1)}, s32[4,3]{1,0:T(4,128)}, u32[]{:S(2)}) copy-start(s32[4,3]{1,0:T(4,128)} %param.11) | copy-start | bytes 148
  102.5 13.1 %copy-start.1 = (bf16[4,2,128,128]{3,2,1,0:T(8,128)(2,1)S(1)}, bf16[4,2,128,128]{3,2,1,0:T(8,128)(2,1)}, u32[]{:S(2)}) copy-start(bf16[4,2,128,128]{3,2,1,0:T(8,128)(2,1)} %param.9) | copy-start | bytes 786436
  102.5 13.1 %copy-start.3 = (bf16[4,128,128]{2,1,0:T(8,128)(2,1)S(1)}, bf16[4,128,128]{2,1,0:T(8,128)(2,1)}, u32[]{:S(2)}) copy-start(bf16[4,128,128]{2,1,0:T(8,128)(2,1)} %param.10) | copy-start | bytes 393220
  104.3 10.4 %all-to-all-start.1 = ((bf16[4,8,1536]{2,0,1:T(4,128)(2,1)}), bf16[4,8,1536]{2,0,1:T(4,128)(2,1)S(1)}, u32[]{:S(2)}, u32[]{:S(2)}) async-start(bf16[4,8,1536]{2,0,1:T(4,128)(2,1)} %copy.77), calls=%async_computation.1 | async-start | bytes 196608 | tf_op jit(solution)/shard_map/all_to_all | solution.py:71
